TPU v7x, 128 devices: a whole 4x4x4 slice. The times are simulated.
128 devices in a mesh: inp: 8 (over z, x_hi), tm: 8 (over x_lo, y), bl: 2 (over core).
Axes of the slice: x: 4 (x_hi: 2, x_lo: 2; x = x_hi * 2 + x_lo), y: 4, z: 4, core: 2. Of those that a mesh axis runs over, the one named last changes fastest.
Arguments:
- voltages: int32 [1024, 524288], P(('inp', 'bl'), 'tm'), may hold values from -16 to 14, as said below
- taps: float32 [4, 16384], replicated, may hold values from -3 to 3
- flags: int32 [1024], P(('inp', 'bl')), may hold values 0 or 1
Outputs:
- visibilities: float32 [2, 128, 8, 128, 1024], P(None, ('inp', 'tm'), None, 'bl')
Inputs may be any that keep to these rules, and one draw needn't show every extreme that they name: `voltages`: int8-valued digitized samples, each input's stream in time order.
All inputs are finite; a program needn't handle non-finite values. No bound on the sum of `flags` on one device may be relied on, other than what follows from the above.
Results may differ from a plain program's by a relative error of at most 0.00065.
Values may be sent and summed in bfloat16 or wider, within the bound.
A program may use at most 192 MiB of HBM per device.

v0:
```python
import math
import jax
import jax.numpy as jnp
from jax import lax
from jax.sharding import PartitionSpec as P

CH_AVG = 64


def passed_along(value, axis, steps):
    count = lax.axis_size(axis)
    initial, last = (max(0, -steps), min(count, count - steps))
    return lax.ppermute(value, axis, [(source, source + steps) for source in range(initial, last)])


def cos_sin(height, breadth, period):
    grid = lax.broadcasted_iota(jnp.int32, (height, breadth), 0) * lax.broadcasted_iota(
        jnp.int32, (height, breadth), 1
    )
    angle = (grid % period).astype(jnp.float32) * (2.0 * math.pi / period)
    return (jnp.cos(angle), jnp.sin(angle))


def transform(filtered, length):
    batch = filtered.shape[0]
    first_len = 128
    second_len = length // first_len
    highest = lax.Precision.HIGHEST
    blocks = filtered.reshape(batch, first_len, second_len)
    cos_one, sin_one = cos_sin(first_len, first_len, first_len)
    table_one = jnp.stack([cos_one, -sin_one])
    section_one = jnp.einsum("ykn,mnb->mykb", table_one, blocks, precision=highest)
    cos_twist, sin_twist = cos_sin(first_len, second_len, length)
    real_one = section_one[:, 0]
    imag_one = section_one[:, 1]
    twisted = jnp.stack(
        [real_one * cos_twist + imag_one * sin_twist, imag_one * cos_twist - real_one * sin_twist],
        axis=1,
    )
    cos_two, sin_two = cos_sin(second_len, second_len // 2, second_len)
    table_two = jnp.stack(
        [jnp.stack([cos_two, -sin_two], axis=1), jnp.stack([sin_two, cos_two], axis=1)]
    )
    result = jnp.einsum("mxkb,xbyq->ymqk", twisted, table_two, precision=highest)
    return result.reshape(2, batch, length // 2)


def shards(voltages, taps, flags):
    inputs = voltages.shape[0]
    tap_count = taps.shape[0]
    length = taps.shape[1]
    spectra_dev = voltages.shape[1] // length
    reach = tap_count - 1
    samples = voltages.astype(jnp.float32).reshape(inputs, spectra_dev, length)
    leading = voltages[:, : reach * length].reshape(inputs, reach, length).astype(jnp.bfloat16)
    following = passed_along(leading, "tm", -1)
    extended = jnp.concatenate([samples, following.astype(jnp.float32)], axis=1)
    filtered = jnp.zeros((inputs, spectra_dev, length), jnp.float32)
    for offset in range(tap_count):
        filtered = (
            filtered + taps[offset][None, None, :] * extended[:, offset : offset + spectra_dev]
        )
    channels = length // 2
    both_parts = transform(filtered.reshape(inputs * spectra_dev, length), length)
    scale = flags.astype(jnp.float32)[None, :, None, None] / (8.0 * math.sqrt(length))
    spectra = (both_parts.reshape(2, inputs, spectra_dev, channels) * scale).astype(jnp.bfloat16)
    turned = lax.all_to_all(
        spectra[:, None], ("inp", "tm"), split_axis=4, concat_axis=1, tiled=True
    )
    groups_inp = lax.axis_size("inp")
    groups_tm = lax.axis_size("tm")
    local_channels = channels // (groups_inp * groups_tm)
    out_groups = local_channels // CH_AVG
    rows = turned.reshape(2, groups_inp, groups_tm, inputs, spectra_dev, out_groups, CH_AVG)
    count = float(groups_tm * spectra_dev * CH_AVG)
    products = jnp.einsum(
        "xatisgk,yctjsgk->gxyaicj",
        rows,
        lax.all_gather(rows, "bl", axis=3, tiled=True),
        preferred_element_type=jnp.float32,
    )
    real_vis = products[:, 0, 0] + products[:, 1, 1]
    imag_vis = products[:, 1, 0] - products[:, 0, 1]
    visibilities = jnp.stack([real_vis, imag_vis]) / count
    return visibilities.reshape(
        2, out_groups, groups_inp, inputs, groups_inp * inputs * lax.axis_size("bl")
    )


def solution(mesh):
    in_specs = (P(("inp", "bl"), "tm"), P(), P(("inp", "bl")))
    out_specs = P(None, ("inp", "tm"), None, "bl", None)
    return jax.shard_map(shards, mesh=mesh, in_specs=in_specs, out_specs=out_specs, check_vma=False)
```

profile of v0, /device:TPU:1, one launch (start us, length us, event | category | flops | bytes accessed | tf_op | source)
XLA Modules:
  0.0 725.3 jit_solution(16236080894492939012)
XLA Ops:
  6.5 0.0 all-gather.2.cloned.1.call-start
  6.5 5.2 slice_convert_fusion
  11.8 3.1 copy.89
  14.9 1.3 collective-permute-start
  16.2 11.3 %convert_element_type.80 = f32[64,65536]{1,0:T(8,128)} convert(s32[64,65536]{1,0:T(8,128)} %param.3) | non-fusion elementwise | flops 4194304 | bytes 33554432 | tf_op jit(solution)/shard_map/convert_element_type | solution.py:54
  27.5 0.0 copy-start.2
  27.5 0.0 copy-start.1
  27.5 17.6 %reshape.218 = f32[64,4,16384]{2,1,0:T(4,128)} reshape(f32[64,65536]{1,0:T(8,128)} %convert_element_type.80) | data formatting | bytes 33554432 | tf_op jit(solution)/shard_map/reshape | solution.py:54
  45.1 0.0 copy-start
  45.1 0.1 fusion.53
  45.2 0.1 fusion.51
  45.4 0.3 sine_negate_fusion
  45.6 0.3 fusion.45
  45.9 0.0 copy-done.2
  46.0 0.0 copy-done.1
  46.0 0.2 fusion.56
  46.2 107.9 %collective-permute-done = bf16[64,3,16384]{2,0,1:T(8,128)(2,1)} collective-permute-done((bf16[64,3,16384]{2,0,1:T(8,128)(2,1)}, bf16[64,3,16384]{2,0,1:T(8,128)(2,1)}, u32[]{:S(2)}, u32[]{:S(2)}) %collective-permute-start) | collective-permute-done | bytes 6291488 | tf_op jit(solution)/shard_map/ppermute | solution.py:13
  154.1 11.2 %copy.53 = f32[64,3,16384]{2,1,0:T(4,128)} copy(bf16[64,3,16384]{2,0,1:T(8,128)(2,1)} %collective-permute-done) | data formatting | bytes 18874368 | tf_op jit(solution)/shard_map/convert_element_type | solution.py:57
  165.3 0.0 copy-done
  165.3 32.6 %fusion.8 = f32[64,4,16384]{2,1,0:T(4,128)} fusion(f32[64,4,16384]{2,1,0:T(4,128)S(1)} %copy-done, f32[64,3,16384]{2,1,0:T(4,128)} %copy.53, f32[16384]{0:T(1024)S(1)} %bitcast.77, f32[16384]{0:T(1024)S(1)} %bitcast.78, f32[16384]{0:T(1024)S(1)} %bitcast.76, f32[16384]{0:T(1024)S(1)} %bitcast.75), kind=kLoop, calls=%fused_computation.13 | loop fusion | flops 41943040 | bytes 46399488 | tf_op jit(solution)/shard_map/add | solution.py:61
  197.9 20.5 %reshape_reshape.6 = f32[256,128,128]{2,1,0:T(8,128)} reshape(f32[64,4,16384]{2,1,0:T(4,128)} %fusion.8) | data formatting | bytes 33554432 | tf_op jit(solution)/shard_map/reshape;reshape | solution.py:29
  218.4 32.5 %fusion.17 = f32[256,2,128,128]{2,3,1,0:T(8,128)} fusion(f32[256,128,128]{2,1,0:T(8,128)} %reshape_reshape.6, f32[1,128,128]{2,1,0:T(8,128)S(1)} %get-tuple-element.15, f32[1,128,128]{2,1,0:T(8,128)S(1)} %get-tuple-element.16), kind=kOutput, calls=%fused_computation.26 | convolution fusion | flops 12884934656 | bytes 50462720 | tf_op jit(solution)/shard_map/ykn,mnb->mykb/dot_general | solution.py:32
  250.8 17.8 %multiply_add_fusion = (f32[256,1,128,128]{2,3,1,0:T(8,128)S(1)}, f32[256,1,128,128]{2,3,1,0:T(8,128)}) fusion(f32[256,2,128,128]{2,3,1,0:T(8,128)} %fusion.17, f32[128,128]{0,1:T(8,128)S(1)} %get-tuple-element.17, f32[128,128]{0,1:T(8,128)S(1)} %get-tuple-element.18), kind=kLoop, calls=%fused_computation.25 | loop fusion | flops 25165824 | bytes 67239936 | tf_op jit(solution)/shard_map/add | solution.py:37
  268.6 23.6 %fusion.25 = f32[2,256,64,128]{3,2,1,0:T(8,128)} fusion(f32[256,1,128,128]{2,3,1,0:T(8,128)} %get-tuple-element.6, f32[256,1,128,128]{2,3,1,0:T(8,128)S(1)} %get-tuple-element.5, f32[1,128,2,64]{1,3,0,2:T(8,128)S(1)} %get-tuple-element.14, f32[1,128,2,64]{1,3,0,2:T(8,128)S(1)} %get-tuple-element.13), kind=kOutput, calls=%fused_computation.30 | convolution fusion | flops 12893323264 | bytes 50462720 | tf_op jit(solution)/shard_map/mxkb,xbyq->ymqk/dot_general | solution.py:44
  292.2 19.9 %reshape_reshape.7 = f32[2,1,64,4,8192]{4,3,2,0,1:T(4,128)} reshape(f32[2,256,64,128]{3,2,1,0:T(8,128)} %fusion.25) | data formatting | bytes 33554432 | tf_op jit(solution)/shard_map/reshape;reshape | solution.py:66
  312.2 16.6 %fusion.16 = bf16[2,1,64,4,8192]{4,2,3,1,0:T(8,128)(2,1)} fusion(f32[2,1,64,4,8192]{4,3,2,0,1:T(4,128)} %reshape_reshape.7, f32[64]{0:T(128)S(1)} %convert_multiply_fusion), kind=kLoop, calls=%fused_computation.23 | loop fusion | flops 8388608 | bytes 25166080 | tf_op jit(solution)/shard_map/convert_element_type | solution.py:66
  328.8 24.4 %copy.57 = bf16[2,1,64,4,8192]{2,3,0,1,4:T(4,128)(2,1)} copy(bf16[2,1,64,4,8192]{4,2,3,1,0:T(8,128)(2,1)} %fusion.16) | data formatting | bytes 16777216 | tf_op jit(solution)/shard_map/convert_element_type | solution.py:66
  353.2 26.5 %reshape.228 = bf16[64,2,32768]{2,1,0:T(2,128)(2,1)} reshape(bf16[8192,1,2,4,64]{4,3,2,1,0:T(4,128)(2,1)} %bitcast.68) | data formatting | bytes 16777216
  379.7 108.5 %all_to_all.15 = bf16[64,2,32768]{2,1,0:T(2,128)(2,1)} all-to-all(bf16[64,2,32768]{2,1,0:T(2,128)(2,1)} %reshape.228), channel_id=1, replica_groups=mesh['inp'=8,'tm'=8,'bl'=2] {'inp','tm'}, dimensions={0} | all-to-all | bytes 16777216 | tf_op jit(solution)/shard_map/all_to_all | solution.py:67
  488.2 26.0 %reshape.229 = bf16[8192,1,2,4,64]{4,3,2,1,0:T(4,128)(2,1)} reshape(bf16[64,2,32768]{2,1,0:T(2,128)(2,1)} %all_to_all.15) | data formatting | bytes 16777216
  514.2 23.4 %copy.77 = bf16[2,1,64,4,64,128]{5,2,3,4,0,1:T(8,128)(2,1)} copy(bf16[2,1,64,4,64,128]{2,3,0,5,4,1:T(4,128)(2,1)} %bitcast.69) | data formatting | bytes 16777216 | tf_op jit(solution)/shard_map/all_to_all | solution.py:67
  537.6 27.8 %reshape.219 = bf16[2,8,8,64,4,2,64]{6,5,3,4,2,1,0:T(2,128)(2,1)} reshape(bf16[2,64,1,64,4,128]{5,3,4,1,0,2:T(8,128)(2,1)} %bitcast.71) | data formatting | bytes 16777216 | tf_op jit(solution)/shard_map/reshape | solution.py:74
  565.4 15.2 %copy.60 = bf16[2,8,8,64,4,2,64]{6,3,2,4,1,0,5:T(8,128)(2,1)} copy(bf16[2,8,8,64,4,2,64]{6,5,3,4,2,1,0:T(2,128)(2,1)} %reshape.219) | data formatting | bytes 16777216 | tf_op jit(solution)/shard_map/reshape | solution.py:74
  580.6 0.0 all-gather.2.cloned.1.call-update
  580.6 54.9 %all-gather.2.cloned.1.call-done = bf16[2,8,8,128,4,2,64]{6,3,2,4,1,0,5:T(8,128)(2,1)} async-done(((bf16[2,8,8,64,4,2,64]{6,3,2,4,1,0,5:T(8,128)(2,1)}), bf16[2,8,8,128,4,2,64]{6,3,2,4,1,0,5:T(8,128)(2,1)}) %all-gather.2.cloned.1.call-update) | async-done | bytes 16777232 | tf_op jit(solution)/shard_map/all_gather | solution.py:79
  635.4 57.3 %fusion.20 = f32[2,2,2,8,64,8,128]{6,4,3,1,5,2,0:T(8,128)} fusion(bf16[2,8,8,64,4,2,64,1,1]{6,5,3,4,2,1,0,8,7:T(2,128)(2,1)} %bitcast.70, bf16[2,8,8,128,4,2,64]{6,3,2,4,1,0,5:T(8,128)(2,1)} %all-gather.2.cloned.1.call-done), kind=kOutput, calls=%fused_computation.29 | convolution fusion | flops 17179869184 | bytes 41943040 | tf_op jit(solution)/shard_map/xatisgk,yctjsgk->gxyaicj/dot_general | solution.py:76
  692.8 10.4 %slice_add_fusion = (f32[2,1,1,8,64,8,128]{6,4,3,1,5,2,0:T(8,128)}, f32[2,1,1,8,64,8,128]{6,4,3,1,5,2,0:T(8,128)S(1)}) fusion(f32[2,2,2,8,64,8,128]{6,4,3,1,5,2,0:T(8,128)} %fusion.20), kind=kLoop, calls=%fused_computation.33 | loop fusion | flops 2097152 | bytes 25165824 | tf_op jit(solution)/shard_map/add | solution.py:82
  703.1 5.5 copy.62
  708.6 1.0 copy.64
  709.6 3.3 copy.63
  712.9 1.0 copy.65
  713.9 4.4 maximum_multiply_fusion
  (2 shorter events, 0.0 us)
Async XLA Ops:
  6.5 628.9 %all-gather.2.cloned.1.call-start = ((), (), s32[]{:S(2)}) async-start(), calls=%async_computation.1 | async-start | bytes 50331648 | tf_op jit(solution)/shard_map/all_gather | solution.py:79
  14.9 139.2 %collective-permute-start = (bf16[64,3,16384]{2,0,1:T(8,128)(2,1)}, bf16[64,3,16384]{2,0,1:T(8,128)(2,1)}, u32[]{:S(2)}, u32[]{:S(2)}) collective-permute-start(bf16[64,3,16384]{2,0,1:T(8,128)(2,1)} %bitcast.67), channel_id=1, source_target_pairs={{2,0},{4,2},{6,4},{8,6},{10,8},{12,10},{14,12},{3,1},{5,3},{7,5},{... | collective-permute-start | bytes 18874376 | tf_op jit(solution)/shard_map/ppermute | solution.py:13
  27.5 18.5 %copy-start.2 = (s32[64]{0:T(128)S(1)}, s32[64]{0:T(128)}, u32[]{:S(2)}) copy-start(s32[64]{0:T(128)} %param.5) | copy-start | bytes 772
  27.5 18.5 %copy-start.1 = (f32[4,16384]{1,0:T(4,128)S(1)}, f32[4,16384]{1,0:T(4,128)}, u32[]{:S(2)}) copy-start(f32[4,16384]{1,0:T(4,128)} %param.4) | copy-start | bytes 786436
  45.1 120.2 %copy-start = (f32[64,4,16384]{2,1,0:T(4,128)S(1)}, f32[64,4,16384]{2,1,0:T(4,128)}, u32[]{:S(2)}) copy-start(f32[64,4,16384]{2,1,0:T(4,128)} %reshape.218) | copy-start | bytes 50331652
Sparse Core Ops, SparseCore 0:
  580.7 54.6 all-gather.1
where the time goes:
time: 737 us; the launch traced here: 725 us
  local copies, waits for them, and re-layouts  227 us (31%)
  waiting for transfers between devices  163 us (22%)
  matrix products  113 us (15%)
  blocking collectives  108 us (15%)
  other arithmetic  99 us (13%)
  between operations  13.7 us (2%)
    all_to_all x1, blocking collectives, shards(): lax.all_to_all(spectra[:, None], ('inp', 'tm'), split_axis=4, concat_axis...  108 us
    ppermute x1, waiting for transfers between devices, passed_along(): lax.ppermute(value, axis, [(source, source + steps) for source in range(i...  108 us
    dot_general x1, matrix products, shards(): jnp.einsum('xatisgk,yctjsgk->gxyaicj', rows, lax.all_gather(rows, 'bl', a...  57.3 us
    all_gather x1, waiting for transfers between devices, shards(): lax.all_gather(rows, 'bl', axis=3, tiled=True)  54.9 us
    unnamed x8, local copies, waits for them, and re-layouts  52.6 us
    reshape x2, local copies, waits for them, and re-layouts, shards(): turned.reshape(2, groups_inp, groups_tm, inputs, spectra_dev, out_groups,...  43 us
    add x1, other arithmetic, shards(): filtered + taps[offset][None, None, :] * extended[:, offset:offset + spec...  32.6 us
    dot_general x1, matrix products, transform(): jnp.einsum('ykn,mnb->mykb', table_one, blocks, precision=highest)  32.5 us
  transfers between devices with their start and end apart: 2, of which 2 were waited for; matrix products, arithmetic and copies ran while one was open for 4% of the time, Pallas kernels for 0%

commit v1 on v0

--- a/solution.py
+++ b/solution.py
@@ -76,7 +76,9 @@
     products = jnp.einsum(
         "xatisgk,yctjsgk->gxyaicj",
         rows,
-        lax.all_gather(rows, "bl", axis=3, tiled=True),
+        jnp.concatenate(
+            lax.all_to_all(jnp.stack([rows] * lax.axis_size("bl")), "bl", 0, 0), axis=3
+        ),
         preferred_element_type=jnp.float32,
     )
     real_vis = products[:, 0, 0] + products[:, 1, 1]

time: 737 us -> 1040 us (1.41)
  local copies, waits for them, and re-layouts: 227 us -> 513 us
  other arithmetic: 99 us -> 159 us
  waiting for transfers between devices: 163 us -> 108 us
  blocking collectives: 108 us -> 143 us
  matrix products: 113 us -> 94.1 us
  between operations: 13.7 us -> 0.57 us
    reshape x0 -> x3, local copies, waits for them, and re-layouts: none -> 203 us  [shards(): jnp.concatenate(lax.all_to_all(jnp.stack([rows] * lax.axis_size('bl')), '...]
    unnamed x8 -> x10, local copies, waits for them, and re-layouts: 52.6 us -> 123 us
    unnamed x0 -> x1, other arithmetic: none -> 60.3 us
    all_gather x1 -> x0, waiting for transfers between devices: 54.9 us -> none  [shards(): lax.all_gather(rows, 'bl', axis=3, tiled=True)]
    all_to_all x0 -> x1, blocking collectives: none -> 34.8 us  [shards(): lax.all_to_all(jnp.stack([rows] * lax.axis_size('bl')), 'bl', 0, 0)]
    another operation x0 -> x1, local copies, waits for them, and re-layouts: none -> 27.8 us  [shards(): jnp.stack([rows] * lax.axis_size('bl'))]
    dot_general x1, matrix products: 57.3 us -> 37.8 us  [shards(): jnp.einsum('xatisgk,yctjsgk->gxyaicj', rows, jnp.concatenate(lax.all_to_a...]
    reshape x2 -> x1, local copies, waits for them, and re-layouts: 43 us -> 27.8 us  [shards(): turned.reshape(2, groups_inp, groups_tm, inputs, spectra_dev, out_groups,...]
  transfers between devices with their start and end apart: 2 -> 1, of which waited for: 2 -> 1; matrix products, arithmetic and copies ran while one was open for 4% -> 3% of each run, Pallas kernels for 0% -> 0%
where the time goes in v1:
time: 1040 us; the launch traced here: 1020 us
  local copies, waits for them, and re-layouts  513 us (49%)
  other arithmetic  159 us (15%)
  blocking collectives  143 us (14%)
  waiting for transfers between devices  108 us (10%)
  matrix products  94.1 us (9%)
    reshape x3, local copies, waits for them, and re-layouts, shards(): jnp.concatenate(lax.all_to_all(jnp.stack([rows] * lax.axis_size('bl')), '...  203 us
    unnamed x10, local copies, waits for them, and re-layouts  123 us
    all_to_all x1, blocking collectives, shards(): lax.all_to_all(spectra[:, None], ('inp', 'tm'), split_axis=4, concat_axis...  108 us
    ppermute x1, waiting for transfers between devices, passed_along(): lax.ppermute(value, axis, [(source, source + steps) for source in range(i...  108 us
    unnamed x1, other arithmetic  60.3 us
    dot_general x1, matrix products, shards(): jnp.einsum('xatisgk,yctjsgk->gxyaicj', rows, jnp.concatenate(lax.all_to_a...  37.8 us
    all_to_all x1, blocking collectives, shards(): lax.all_to_all(jnp.stack([rows] * lax.axis_size('bl')), 'bl', 0, 0)  34.8 us
    add x1, other arithmetic, shards(): filtered + taps[offset][None, None, :] * extended[:, offset:offset + spec...  32.6 us
  transfers between devices with their start and end apart: 1, of which 1 were waited for; matrix products, arithmetic and copies ran while one was open for 3% of the time, Pallas kernels for 0%

profile of v1, /device:TPU:1, one launch (start us, length us, event | category | flops | bytes accessed | tf_op | source)
XLA Modules:
  0.0 1018.8 jit_solution(957770780570440682)
XLA Ops:
  0.0 5.2 slice_convert_fusion
  5.2 3.1 copy.94
  8.4 1.3 collective-permute-start
  9.6 11.3 %convert_element_type.80 = f32[64,65536]{1,0:T(8,128)} convert(s32[64,65536]{1,0:T(8,128)} %param.3) | non-fusion elementwise | flops 4194304 | bytes 33554432 | tf_op jit(solution)/shard_map/convert_element_type | solution.py:54
  20.9 0.0 copy-start.2
  20.9 0.0 copy-start.1
  20.9 17.6 %reshape.225 = f32[64,4,16384]{2,1,0:T(4,128)} reshape(f32[64,65536]{1,0:T(8,128)} %convert_element_type.80) | data formatting | bytes 33554432 | tf_op jit(solution)/shard_map/reshape | solution.py:54
  38.5 0.0 copy-start
  38.5 0.1 fusion.53
  38.7 0.1 fusion.51
  38.8 0.3 sine_negate_fusion
  39.1 0.3 fusion.45
  39.4 0.0 copy-done.2
  39.4 0.0 copy-done.1
  39.4 0.2 fusion.56
  39.6 107.9 %collective-permute-done = bf16[64,3,16384]{2,0,1:T(8,128)(2,1)} collective-permute-done((bf16[64,3,16384]{2,0,1:T(8,128)(2,1)}, bf16[64,3,16384]{2,0,1:T(8,128)(2,1)}, u32[]{:S(2)}, u32[]{:S(2)}) %collective-permute-start) | collective-permute-done | bytes 6291488 | tf_op jit(solution)/shard_map/ppermute | solution.py:13
  147.5 11.2 %copy.56 = f32[64,3,16384]{2,1,0:T(4,128)} copy(bf16[64,3,16384]{2,0,1:T(8,128)(2,1)} %collective-permute-done) | data formatting | bytes 18874368 | tf_op jit(solution)/shard_map/convert_element_type | solution.py:57
  158.8 0.0 copy-done
  158.8 32.6 %fusion.6 = f32[64,4,16384]{2,1,0:T(4,128)} fusion(f32[64,4,16384]{2,1,0:T(4,128)S(1)} %copy-done, f32[64,3,16384]{2,1,0:T(4,128)} %copy.56, f32[16384]{0:T(1024)S(1)} %bitcast.89, f32[16384]{0:T(1024)S(1)} %bitcast.90, f32[16384]{0:T(1024)S(1)} %bitcast.88, f32[16384]{0:T(1024)S(1)} %bitcast.87), kind=kLoop, calls=%fused_computation.12 | loop fusion | flops 41943040 | bytes 46399488 | tf_op jit(solution)/shard_map/add | solution.py:61
  191.4 20.5 %reshape_reshape.6 = f32[256,128,128]{2,1,0:T(8,128)} reshape(f32[64,4,16384]{2,1,0:T(4,128)} %fusion.6) | data formatting | bytes 33554432 | tf_op jit(solution)/shard_map/reshape;reshape | solution.py:29
  211.9 32.5 %fusion.17 = f32[256,2,128,128]{2,3,1,0:T(8,128)} fusion(f32[256,128,128]{2,1,0:T(8,128)} %reshape_reshape.6, f32[1,128,128]{2,1,0:T(8,128)S(1)} %get-tuple-element.15, f32[1,128,128]{2,1,0:T(8,128)S(1)} %get-tuple-element.16), kind=kOutput, calls=%fused_computation.27 | convolution fusion | flops 12884934656 | bytes 50462720 | tf_op jit(solution)/shard_map/ykn,mnb->mykb/dot_general | solution.py:32
  244.4 17.7 %multiply_add_fusion = (f32[256,1,128,128]{2,3,1,0:T(8,128)S(1)}, f32[256,1,128,128]{2,3,1,0:T(8,128)}) fusion(f32[256,2,128,128]{2,3,1,0:T(8,128)} %fusion.17, f32[128,128]{0,1:T(8,128)S(1)} %get-tuple-element.17, f32[128,128]{0,1:T(8,128)S(1)} %get-tuple-element.18), kind=kLoop, calls=%fused_computation.26 | loop fusion | flops 25165824 | bytes 67239936 | tf_op jit(solution)/shard_map/add | solution.py:37
  262.1 23.8 %fusion.25 = f32[2,256,64,128]{3,2,1,0:T(8,128)} fusion(f32[256,1,128,128]{2,3,1,0:T(8,128)} %get-tuple-element.6, f32[256,1,128,128]{2,3,1,0:T(8,128)S(1)} %get-tuple-element.5, f32[1,128,2,64]{1,3,0,2:T(8,128)S(1)} %get-tuple-element.14, f32[1,128,2,64]{1,3,0,2:T(8,128)S(1)} %get-tuple-element.13), kind=kOutput, calls=%fused_computation.31 | convolution fusion | flops 12893323264 | bytes 50462720 | tf_op jit(solution)/shard_map/mxkb,xbyq->ymqk/dot_general | solution.py:44
  285.9 19.9 %reshape_reshape.7 = f32[2,1,64,4,8192]{4,3,2,0,1:T(4,128)} reshape(f32[2,256,64,128]{3,2,1,0:T(8,128)} %fusion.25) | data formatting | bytes 33554432 | tf_op jit(solution)/shard_map/reshape;reshape | solution.py:66
  305.8 16.6 %fusion.16 = bf16[2,1,64,4,8192]{4,2,3,1,0:T(8,128)(2,1)} fusion(f32[2,1,64,4,8192]{4,3,2,0,1:T(4,128)} %reshape_reshape.7, f32[64]{0:T(128)S(1)} %convert_multiply_fusion), kind=kLoop, calls=%fused_computation.24 | loop fusion | flops 8388608 | bytes 25166080 | tf_op jit(solution)/shard_map/convert_element_type | solution.py:66
  322.4 24.4 %copy.60 = bf16[2,1,64,4,8192]{2,3,0,1,4:T(4,128)(2,1)} copy(bf16[2,1,64,4,8192]{4,2,3,1,0:T(8,128)(2,1)} %fusion.16) | data formatting | bytes 16777216 | tf_op jit(solution)/shard_map/convert_element_type | solution.py:66
  346.9 26.5 %reshape.238 = bf16[64,2,32768]{2,1,0:T(2,128)(2,1)} reshape(bf16[8192,1,2,4,64]{4,3,2,1,0:T(4,128)(2,1)} %bitcast.81) | data formatting | bytes 16777216
  373.4 108.2 %all_to_all.20 = bf16[64,2,32768]{2,1,0:T(2,128)(2,1)} all-to-all(bf16[64,2,32768]{2,1,0:T(2,128)(2,1)} %reshape.238), channel_id=1, replica_groups=mesh['inp'=8,'tm'=8,'bl'=2] {'inp','tm'}, dimensions={0} | all-to-all | bytes 16777216 | tf_op jit(solution)/shard_map/all_to_all | solution.py:67
  481.6 26.0 %reshape.239 = bf16[8192,1,2,4,64]{4,3,2,1,0:T(4,128)(2,1)} reshape(bf16[64,2,32768]{2,1,0:T(2,128)(2,1)} %all_to_all.20) | data formatting | bytes 16777216
  507.5 23.4 %copy.81 = bf16[2,1,64,4,64,128]{5,2,3,4,0,1:T(8,128)(2,1)} copy(bf16[2,1,64,4,64,128]{2,3,0,5,4,1:T(4,128)(2,1)} %bitcast.82) | data formatting | bytes 16777216 | tf_op jit(solution)/shard_map/all_to_all | solution.py:67
  530.9 27.8 %stack_reshape.4 = bf16[1,2,8,8,64,4,2,64]{7,6,4,5,3,2,1,0:T(2,128)(2,1)} reshape(bf16[2,64,1,64,4,128]{5,3,4,1,0,2:T(8,128)(2,1)} %bitcast.79) | data formatting | bytes 16777216 | tf_op jit(solution)/shard_map/stack;reshape | solution.py:80
  558.7 27.8 %reshape.228 = bf16[2,8,8,64,4,2,64]{6,5,3,4,2,1,0:T(2,128)(2,1)} reshape(bf16[2,64,1,64,4,128]{5,3,4,1,0,2:T(8,128)(2,1)} %bitcast.80) | data formatting | bytes 16777216 | tf_op jit(solution)/shard_map/reshape | solution.py:74
  586.6 60.3 %fusion.57 = bf16[2,2,8,8,4,64,2,64]{7,6,5,4,3,2,1,0:T(2,128)(2,1)} fusion(bf16[1,2,8,8,64,4,2,64]{7,6,4,5,3,2,1,0:T(2,128)(2,1)} %stack_reshape.4), kind=kLoop, calls=%fused_computation.81 | loop fusion | flops 8388608 | bytes 25165824
  646.8 27.6 %reshape.240 = bf16[2,2,2097152]{2,1,0:T(2,128)(2,1)} reshape(bf16[2,2,8,8,4,64,2,64]{7,6,5,4,3,2,1,0:T(2,128)(2,1)} %fusion.57) | data formatting | bytes 33554432
  674.4 34.8 %all_to_all.21 = bf16[2,2,2097152]{2,1,0:T(2,128)(2,1)} all-to-all(bf16[2,2,2097152]{2,1,0:T(2,128)(2,1)} %reshape.240), channel_id=1, replica_groups=mesh['inp'=8,'tm'=8,'bl'=2] {'bl'}, dimensions={0} | all-to-all | bytes 33554432 | tf_op jit(solution)/shard_map/all_to_all | solution.py:80
  709.2 43.1 %reshape.241 = bf16[2,2,8,8,4,64,2,64]{7,6,5,4,3,2,1,0:T(2,128)(2,1)} reshape(bf16[2,2,2097152]{2,1,0:T(2,128)(2,1)} %all_to_all.21) | data formatting | bytes 33554432
  752.3 28.9 %bitcast_bitcast_fusion = bf16[2,8,8,2,64,4,2,64]{7,6,4,5,2,1,0,3:T(2,128)(2,1)} fusion(bf16[2,2,8,8,4,64,2,64]{7,6,5,4,3,2,1,0:T(2,128)(2,1)} %reshape.241), kind=kLoop, calls=%fused_computation.82 | loop fusion | bytes 33554432 | tf_op jit(solution)/shard_map/reshape | solution.py:79
  781.2 121.3 %copy.63 = bf16[2,8,8,2,64,4,2,64]{4,3,7,2,5,1,0,6:T(2,128)(2,1)} copy(bf16[2,8,8,2,64,4,2,64]{7,6,4,5,2,1,0,3:T(2,128)(2,1)} %bitcast_bitcast_fusion) | data formatting | bytes 33554432 | tf_op jit(solution)/shard_map/reshape | solution.py:79
  902.5 52.4 %reshape.234 = bf16[2,8,8,128,4,2,64,1,1]{3,6,2,4,1,0,5,7,8:T(8,128)(2,1)} reshape(bf16[2,8,8,2,64,4,2,64]{4,3,7,2,5,1,0,6:T(2,128)(2,1)} %copy.63) | data formatting | bytes 33554432 | tf_op jit(solution)/shard_map/reshape | solution.py:79
  955.0 37.8 %fusion.20 = f32[2,2,2,8,64,8,128]{6,4,3,1,5,2,0:T(8,128)} fusion(bf16[2,8,8,64,4,2,64,1,1]{6,5,3,4,2,1,0,8,7:T(2,128)(2,1)} %bitcast.84, bf16[2,8,8,128,4,2,64,1,1]{3,6,2,4,1,0,5,7,8:T(8,128)(2,1)} %reshape.234), kind=kOutput, calls=%fused_computation.30 | convolution fusion | flops 17179869184 | bytes 41943040 | tf_op jit(solution)/shard_map/xatisgk,yctjsgk->gxyaicj/dot_general | solution.py:76
  992.8 10.4 %slice_add_fusion = (f32[2,1,1,8,64,8,128]{6,4,3,1,5,2,0:T(8,128)}, f32[2,1,1,8,64,8,128]{6,4,3,1,5,2,0:T(8,128)S(1)}) fusion(f32[2,2,2,8,64,8,128]{6,4,3,1,5,2,0:T(8,128)} %fusion.20), kind=kLoop, calls=%fused_computation.34 | loop fusion | flops 2097152 | bytes 25165824 | tf_op jit(solution)/shard_map/add | solution.py:84
  1003.1 5.5 copy.66
  1008.6 1.0 copy.68
  1009.6 3.3 copy.67
  1012.9 1.0 copy.69
  1013.9 4.4 maximum_multiply_fusion
  (2 shorter events, 0.0 us)
Async XLA Ops:
  8.4 139.2 %collective-permute-start = (bf16[64,3,16384]{2,0,1:T(8,128)(2,1)}, bf16[64,3,16384]{2,0,1:T(8,128)(2,1)}, u32[]{:S(2)}, u32[]{:S(2)}) collective-permute-start(bf16[64,3,16384]{2,0,1:T(8,128)(2,1)} %bitcast.78), channel_id=1, source_target_pairs={{2,0},{4,2},{6,4},{8,6},{10,8},{12,10},{14,12},{3,1},{5,3},{7,5},{... | collective-permute-start | bytes 18874376 | tf_op jit(solution)/shard_map/ppermute | solution.py:13
  20.9 18.5 %copy-start.2 = (s32[64]{0:T(128)S(1)}, s32[64]{0:T(128)}, u32[]{:S(2)}) copy-start(s32[64]{0:T(128)} %param.5) | copy-start | bytes 772
  20.9 18.5 %copy-start.1 = (f32[4,16384]{1,0:T(4,128)S(1)}, f32[4,16384]{1,0:T(4,128)}, u32[]{:S(2)}) copy-start(f32[4,16384]{1,0:T(4,128)} %param.4) | copy-start | bytes 786436
  38.5 120.2 %copy-start = (f32[64,4,16384]{2,1,0:T(4,128)S(1)}, f32[64,4,16384]{2,1,0:T(4,128)}, u32[]{:S(2)}) copy-start(f32[64,4,16384]{2,1,0:T(4,128)} %reshape.225) | copy-start | bytes 50331652
